TPU v7x, 512 devices: a whole 4x8x8 slice. The times are simulated.
512 devices in a mesh: rep: 8 (over z_hi, core), dp: 64 (over z_lo, x, y).
Axes of the slice: x: 4, y: 8, z: 8 (z_hi: 4, z_lo: 2; z = z_hi * 2 + z_lo), core: 2. Of those that a mesh axis runs over, the one named last changes fastest.
Arguments:
- frames: bfloat16 [98304, 1536], P(('rep', 'dp')), may hold values from -6 to 6
- lengths: int32 [512, 8], P(('rep', 'dp')), may hold values from 0 to 192, as said below
- destination: int32 [512, 48], P(('rep', 'dp')), may hold values from -1 to 63, as said below
- kernel: float32 [15, 1536], replicated, may hold values from -1.5 to 1.5
- norm_gain: float32 [1536], replicated, may hold values from 0.5 to 1.5
- master: float32 [1536, 1536], P('dp'), may hold values from -0.15625 to 0.15625
- moment: float32 [1536, 1536], P('dp'), may hold values from -0.18 to 0.18
- second: float32 [1536, 1536], P('dp'), may hold values from 0.0003 to 0.003
- gradient: float32 [1536, 1536], P('dp'), may hold values from -1.8 to 1.8
- bucket_order: int32 [64], replicated, may hold values from 0 to 63, each once
- cotangent: bfloat16 [65536, 1536], P(('rep', 'dp')), may hold values from -6 to 6
Outputs:
- projected: bfloat16 [65536, 1536], P(('rep', 'dp'))
- frame_grad: bfloat16 [98304, 1536], P(('rep', 'dp'))
- kernel_grad: float32 [15, 1536], replicated
- gain_grad: float32 [1536], replicated
- new_master: float32 [1536, 1536], P('dp')
Inputs may be any that keep to these rules, and one draw needn't show every extreme that they name: destination[i, b] is the device of i's replica group that takes block b of device i, or -1 for a block without frames; a device's blocks with frames come first and go to distinct devices; every device receives exactly 32 blocks. A device's lengths add up to 4 times the number of its blocks that destination sends.
All inputs are finite; a program needn't handle non-finite values.
Results may differ from a plain program's by a relative error of at most 0.012.
Values may be sent and summed in bfloat16 or wider, within the bound.
No kernel may reach another device: no remote copies, remote signals or barrier semaphores. Data moves between devices by JAX's collectives and lax.ppermute only.
A program may use at most 128 MiB of HBM per device.

v0:
```python
import math
import jax
import jax.numpy as jnp
from jax import lax
from jax.sharding import PartitionSpec as P

ROWS = 128


def adam_step(master, moment, second, gradient):
    moment_new = 0.9 * moment + 0.1 * gradient
    second_new = 0.999 * second + 0.001 * jnp.square(gradient)
    return master - 0.01 * (moment_new / (jnp.sqrt(second_new) + 1e-08) + 0.1 * master)


def layout(lengths_row, height):
    bounds = jnp.cumsum(lengths_row)
    position = jnp.arange(height, dtype=jnp.int32)
    segment = jnp.sum((position[:, None] >= bounds[None, :]).astype(jnp.int32), axis=1)
    living = (position < bounds[-1]).astype(jnp.float32)
    return (segment, living)


def activate(frames_f, kernel, norm_gain, segment, living):
    height = frames_f.shape[0]
    half_width = (kernel.shape[0] - 1) // 2
    padded = jnp.pad(frames_f, ((half_width, half_width), (0, 0)))
    padded_seg = jnp.pad(segment, (half_width, half_width), constant_values=-1)
    mixed_sum = jnp.zeros_like(frames_f)
    for tap_index in range(kernel.shape[0]):
        inside = (lax.slice_in_dim(padded_seg, tap_index, tap_index + height) == segment).astype(
            frames_f.dtype
        )
        mixed_sum = (
            mixed_sum
            + kernel[tap_index]
            * lax.slice_in_dim(padded, tap_index, tap_index + height)
            * inside[:, None]
        )
    mixed_sum = mixed_sum * living[:, None]
    center = jnp.mean(mixed_sum, axis=1, keepdims=True)
    spread = jnp.mean(jnp.square(mixed_sum - center), axis=1, keepdims=True)
    scaled = (mixed_sum - center) * lax.rsqrt(spread + 1e-05) * norm_gain
    return scaled * jax.nn.sigmoid(scaled)


def to_owners(payload, sending, has_block, blocks, block_rows, received_blocks):
    columns = payload.shape[1]
    outgoing = jnp.einsum(
        "pn,nf->pf",
        sending,
        payload.reshape(blocks, block_rows * columns),
        preferred_element_type=jnp.float32,
    ).astype(jnp.bfloat16)
    incoming, arrived = (
        lax.all_to_all(outgoing, "dp", split_axis=0, concat_axis=0, tiled=True),
        lax.all_to_all(has_block, "dp", split_axis=0, concat_axis=0, tiled=True),
    )
    arrived_flag = arrived[:, 0].astype(jnp.float32)
    ranking = jnp.cumsum(arrived_flag) - 1.0
    wanted = jnp.arange(received_blocks).astype(jnp.float32)
    picking = ((ranking[None, :] == wanted[:, None]) & (arrived_flag[None, :] > 0.5)).astype(
        jnp.bfloat16
    )
    compact = jnp.einsum("mp,pf->mf", picking, incoming, preferred_element_type=jnp.float32).astype(
        jnp.bfloat16
    )
    return (compact.reshape(received_blocks * block_rows, columns), picking)


def to_sources(payload, picking, sending, blocks, block_rows, received_blocks):
    columns = payload.shape[1]
    outgoing = jnp.einsum(
        "mp,mf->pf",
        picking,
        payload.reshape(received_blocks, block_rows * columns),
        preferred_element_type=jnp.float32,
    ).astype(jnp.bfloat16)
    incoming = lax.all_to_all(outgoing, "dp", split_axis=0, concat_axis=0, tiled=True)
    homed = jnp.einsum("pn,pf->nf", sending, incoming, preferred_element_type=jnp.float32).astype(
        jnp.bfloat16
    )
    return homed.reshape(blocks * block_rows, columns)


def body(
    frames,
    lengths,
    destination,
    kernel,
    norm_gain,
    master,
    moment,
    second,
    gradient,
    bucket_order,
    cotangent,
):
    owners = lax.axis_size("dp")
    columns = frames.shape[1]
    updated = adam_step(master, moment, second, gradient)
    bucket = updated.astype(jnp.bfloat16)
    bucket_rows = bucket.shape[0]
    gathered = lax.all_gather(bucket, "dp", axis=0, tiled=True)
    weight = jnp.take(gathered.reshape(owners, bucket_rows, columns), bucket_order, axis=0).reshape(
        owners * bucket_rows, columns
    )
    height = frames.shape[0]
    blocks = destination.shape[1]
    block_rows = height // blocks
    received_blocks = cotangent.shape[0] // block_rows
    segment, living = layout(lengths[0], height)
    activated, pullback = jax.vjp(
        lambda inputs, kernel_in, gain_in: activate(inputs, kernel_in, gain_in, segment, living),
        frames.astype(jnp.float32),
        kernel,
        norm_gain,
    )
    moved_rows = activated.astype(jnp.bfloat16)
    targets = jnp.arange(owners, dtype=jnp.int32)
    sending = (destination[0][None, :] == targets[:, None]).astype(jnp.bfloat16)
    has_block = jnp.sum(sending, axis=1, keepdims=True)
    dims_back = (((1,), (1,)), ((), ()))
    source_proj = jnp.dot(moved_rows, weight, preferred_element_type=jnp.float32).astype(
        jnp.bfloat16
    )
    projected, picking = to_owners(
        source_proj, sending, has_block, blocks, block_rows, received_blocks
    )
    cot_home = to_sources(cotangent, picking, sending, blocks, block_rows, received_blocks)
    returned = lax.dot_general(
        cot_home, weight, dims_back, preferred_element_type=jnp.float32
    ).astype(jnp.bfloat16)
    frame_term, kernel_term, gain_term = pullback(returned.astype(jnp.float32))
    kernel_total, gain_total = lax.psum((kernel_term, gain_term), ("rep", "dp"))
    divisor = math.sqrt(lax.axis_size("rep") * owners * ROWS)
    return (
        projected,
        frame_term.astype(jnp.bfloat16),
        kernel_total / divisor,
        gain_total / divisor,
        updated,
    )


def solution(mesh):
    return jax.shard_map(
        body,
        mesh=mesh,
        in_specs=(
            P(("rep", "dp"), None),
            P(("rep", "dp"), None),
            P(("rep", "dp"), None),
            P(),
            P(),
            P("dp", None),
            P("dp", None),
            P("dp", None),
            P("dp", None),
            P(),
            P(("rep", "dp"), None),
        ),
        out_specs=(P(("rep", "dp"), None), P(("rep", "dp"), None), P(), P(), P("dp", None)),
        check_vma=False,
    )
```

profile of v0, /device:TPU:1, one launch (start us, length us, event | category | flops | bytes accessed | tf_op | source)
XLA Modules:
  0.0 658.0 jit_solution(7766027091813819460)
XLA Ops:
  7.2 2.0 fusion.27
  10.7 12.9 %all-to-all-start = ((bf16[64,1,1]{2,1,0:T(2,128)(2,1)}), bf16[64,1,1]{2,1,0:T(2,128)(2,1)S(1)}, u32[]{:S(2)}, u32[]{:S(2)}) async-start(bf16[64,1,1]{2,1,0:T(2,128)(2,1)} %copy.26), calls=%async_computation | async-start | bytes 65536 | tf_op jit(solution)/shard_map/all_to_all | solution.py:57
  29.6 3.3 all-to-all-done
  38.6 7.8 %all-to-all-start.2 = ((bf16[64,2,3072]{2,1,0:T(2,128)(2,1)}), bf16[64,2,3072]{2,1,0:T(2,128)(2,1)S(1)}, u32[]{:S(2)}, u32[]{:S(2)}) async-start(bf16[64,2,3072]{2,1,0:T(2,128)(2,1)} %reshape.312), calls=%async_computation.2 | async-start | bytes 1572864 | tf_op jit(solution)/shard_map/all_to_all | solution.py:79
  47.0 3.9 fusion.26
  52.0 19.9 %all-to-all-done.2 = bf16[64,2,3072]{2,1,0:T(2,128)(2,1)S(1)} async-done(((bf16[64,2,3072]{2,1,0:T(2,128)(2,1)}), bf16[64,2,3072]{2,1,0:T(2,128)(2,1)S(1)}, u32[]{:S(2)}, u32[]{:S(2)}) %all-to-all-start.2) | async-done | bytes 786464 | tf_op jit(solution)/shard_map/all_to_all | solution.py:79
  71.9 2.0 reshape.313
  73.8 2.1 convolution_convert_fusion.2
  77.1 206.7 %all-gather.2.cloned.1.call-done = bf16[1536,1536]{1,0:T(8,128)(2,1)} async-done(((bf16[24,1536]{1,0:T(8,128)(2,1)}), bf16[1536,1536]{1,0:T(8,128)(2,1)}) %all-gather.2.cloned.1.call-update) | async-done | bytes 4718608 | tf_op jit(solution)/shard_map/all_gather | solution.py:104
  283.8 5.4 gather_fusion
  289.3 2.9 broadcast_select_fusion
  292.2 2.6 multiply_reduce_fusion
  295.7 3.6 multiply_reduce_fusion.15
  299.4 4.3 multiply_reduce_fusion.5
  303.8 4.6 multiply_multiply_fusion.13
  309.3 2.0 convolution_convert_fusion.5
  311.4 2.3 reshape.264
  320.7 1.8 reduce.35
  322.5 3.2 reshape.310
  325.7 7.3 %all-to-all-start.1 = ((bf16[64,2,3072]{2,1,0:T(2,128)(2,1)}), bf16[64,2,3072]{2,1,0:T(2,128)(2,1)}, u32[]{:S(2)}, u32[]{:S(2)}) async-start(bf16[64,2,3072]{2,1,0:T(2,128)(2,1)} %reshape.310), calls=%async_computation.1 | async-start | bytes 1572864 | tf_op jit(solution)/shard_map/all_to_all | solution.py:56
  337.5 142.7 %psum.15 = f32[1536]{0:T(1024)S(1)} all-reduce(f32[1536]{0:T(1024)} %get-tuple-element.5), channel_id=1, replica_groups=mesh['rep'=8,'dp'=64] {'rep','dp'}, use_global_device_ids=true, to_apply=%region_26.27 | all-reduce | flops 1536 | bytes 12288 | tf_op jit(solution)/shard_map/psum | solution.py:135
  480.3 5.0 pad_add_fusion
  487.6 155.4 %all-reduce.34.cloned.1.call-done = f32[15,1536]{1,0:T(8,128)} async-done(((f32[15,1536]{1,0:T(8,128)}), f32[15,1536]{1,0:T(8,128)}) %all-reduce.34.cloned.1.call-update) | async-done | bytes 92176 | tf_op jit(solution)/shard_map/psum | solution.py:135
  644.6 4.9 reshape.311
  (254 shorter events, 34.2 us)
Async XLA Ops:
  7.2 22.0 %copy-start.9 = (bf16[128,1536]{1,0:T(8,128)(2,1)S(1)}, bf16[128,1536]{1,0:T(8,128)(2,1)}, u32[]{:S(2)}) copy-start(bf16[128,1536]{1,0:T(8,128)(2,1)} %param.21) | copy-start | bytes 1179652
  7.2 22.3 %copy-start.6 = (bf16[192,1536]{1,0:T(8,128)(2,1)S(1)}, bf16[192,1536]{1,0:T(8,128)(2,1)}, u32[]{:S(2)}) copy-start(bf16[192,1536]{1,0:T(8,128)(2,1)} %param.11) | copy-start | bytes 1769476
  7.2 276.6 %all-gather.2.cloned.1.call-start = ((), (), s32[]{:S(2)}) async-start(), calls=%async_computation.3 | async-start | bytes 4792320 | tf_op jit(solution)/shard_map/all_gather | solution.py:104
  10.7 22.2 %all-to-all-start = ((bf16[64,1,1]{2,1,0:T(2,128)(2,1)}), bf16[64,1,1]{2,1,0:T(2,128)(2,1)S(1)}, u32[]{:S(2)}, u32[]{:S(2)}) async-start(bf16[64,1,1]{2,1,0:T(2,128)(2,1)} %copy.26), calls=%async_computation | async-start | bytes 65536 | tf_op jit(solution)/shard_map/all_to_all | solution.py:57
  25.1 9.3 %copy-start.91 = (f32[32]{0:T(128)}, f32[32]{0:T(128)S(1)}, u32[]{:S(2)}) copy-start(f32[32]{0:T(128)S(1)} %iota_convert_fusion) | copy-start | bytes 388
  38.5 7.9 %copy-start.10 = (f32[15,1536]{1,0:T(8,128)S(1)}, f32[15,1536]{1,0:T(8,128)}, u32[]{:S(2)}) copy-start(f32[15,1536]{1,0:T(8,128)} %param.14) | copy-start | bytes 276484
  38.5 8.4 %copy-start.48 = (f32[192]{0:T(256)S(1)}, f32[192]{0:T(256)}, u32[]{:S(2)}) copy-start(f32[192]{0:T(256)} %get-tuple-element.71) | copy-start | bytes 2308
  38.5 8.4 %copy-start.68 = (f32[192]{0:T(256)S(1)}, f32[192]{0:T(256)}, u32[]{:S(2)}) copy-start(f32[192]{0:T(256)} %get-tuple-element.67) | copy-start | bytes 2308
  38.5 8.4 %copy-start.70 = (f32[192]{0:T(256)S(1)}, f32[192]{0:T(256)}, u32[]{:S(2)}) copy-start(f32[192]{0:T(256)} %get-tuple-element.68) | copy-start | bytes 2308
  38.5 8.5 %copy-start.72 = (f32[192]{0:T(256)S(1)}, f32[192]{0:T(256)}, u32[]{:S(2)}) copy-start(f32[192]{0:T(256)} %get-tuple-element.69) | copy-start | bytes 2308
  38.6 8.5 %copy-start.74 = (f32[192]{0:T(256)S(1)}, f32[192]{0:T(256)}, u32[]{:S(2)}) copy-start(f32[192]{0:T(256)} %get-tuple-element.70) | copy-start | bytes 2308
  38.6 8.5 %copy-start.76 = (f32[192]{0:T(256)S(1)}, f32[192]{0:T(256)}, u32[]{:S(2)}) copy-start(f32[192]{0:T(256)} %get-tuple-element.73) | copy-start | bytes 2308
  38.6 33.3 %all-to-all-start.2 = ((bf16[64,2,3072]{2,1,0:T(2,128)(2,1)}), bf16[64,2,3072]{2,1,0:T(2,128)(2,1)S(1)}, u32[]{:S(2)}, u32[]{:S(2)}) async-start(bf16[64,2,3072]{2,1,0:T(2,128)(2,1)} %reshape.312), calls=%async_computation.2 | async-start | bytes 1572864 | tf_op jit(solution)/shard_map/all_to_all | solution.py:79
  51.1 22.7 %copy-start.66 = (f32[192]{0:T(256)}, f32[192]{0:T(256)S(1)}, u32[]{:S(2)}) copy-start(f32[192]{0:T(256)S(1)} %broadcast_multiply_fusion.3) | copy-start | bytes 2308
  51.4 22.4 %copy-start.80 = (f32[192]{0:T(256)}, f32[192]{0:T(256)S(1)}, u32[]{:S(2)}) copy-start(f32[192]{0:T(256)S(1)} %multiply_reduce_fusion.17) | copy-start | bytes 2308
  52.0 21.9 %copy-start.89 = (s32[1,48]{1,0:T(1,128)S(1)}, s32[1,48]{1,0:T(1,128)}, u32[]{:S(2)}) copy-start(s32[1,48]{1,0:T(1,128)} %param.13) | copy-start | bytes 580
  299.4 9.0 %slice-start = ((s8[4718592]{0:T(1024)(128)(4,1)}), s8[4194304]{0:T(1024)(128)(4,1)S(1)}, s32[]{:S(2)}) async-start(s8[4718592]{0:T(1024)(128)(4,1)} %bitcast.25), calls=%async_computation.5 | async-start | bytes 8388608
  311.4 7.2 %copy-start.39 = (f32[1536]{0:T(1024)S(1)}, f32[1536]{0:T(1024)}, u32[]{:S(2)}) copy-start(f32[1536]{0:T(1024)} %get-tuple-element.15) | copy-start | bytes 18436
  311.4 7.8 %copy-start.90 = (s32[1,48]{1,0:T(1,128)S(1)}, s32[1,48]{1,0:T(1,128)}, u32[]{:S(2)}) copy-start(s32[1,48]{1,0:T(1,128)} %param.13) | copy-start | bytes 580
  325.7 10.2 %copy-start.38 = (f32[1536]{0:T(1024)S(1)}, f32[1536]{0:T(1024)}, u32[]{:S(2)}) copy-start(f32[1536]{0:T(1024)} %get-tuple-element.20) | copy-start | bytes 18436
  325.7 10.2 %copy-start.37 = (f32[1536]{0:T(1024)S(1)}, f32[1536]{0:T(1024)}, u32[]{:S(2)}) copy-start(f32[1536]{0:T(1024)} %get-tuple-element.22) | copy-start | bytes 18436
  325.7 154.5 %copy-start = (f32[192,1536]{1,0:T(8,128)S(1)}, f32[192,1536]{1,0:T(8,128)}, u32[]{:S(2)}) copy-start(f32[192,1536]{1,0:T(8,128)} %get-tuple-element.50) | copy-start | bytes 3538948
  325.7 318.9 %all-to-all-start.1 = ((bf16[64,2,3072]{2,1,0:T(2,128)(2,1)}), bf16[64,2,3072]{2,1,0:T(2,128)(2,1)}, u32[]{:S(2)}, u32[]{:S(2)}) async-start(bf16[64,2,3072]{2,1,0:T(2,128)(2,1)} %reshape.310), calls=%async_computation.1 | async-start | bytes 1572864 | tf_op jit(solution)/shard_map/all_to_all | solution.py:56
  333.0 310.1 %all-reduce.34.cloned.1.call-start = ((), (), s32[]{:S(2)}) async-start(), calls=%async_computation.4 | async-start | bytes 196608 | tf_op jit(solution)/shard_map/psum | solution.py:135
  (78 other events, 285.1 us)
Sparse Core Ops, SparseCore 0:
  10.7 273.0 all-gather.1
  339.4 303.6 all-reduce.33
where the time goes:
time: 659 us; the launch traced here: 658 us
  waiting for transfers between devices  385 us (58%)
  blocking collectives  143 us (22%)
  other arithmetic  43.2 us (7%)
  local copies, waits for them, and re-layouts  34.2 us (5%)
  starting transfers between devices  28.1 us (4%)
  between operations  15.3 us (2%)
  matrix products  9.28 us (1%)
    all_gather x1, waiting for transfers between devices, body(): gathered = lax.all_gather(bucket, 'dp', axis=0, tiled=True)  207 us
    psum x1, waiting for transfers between devices, body(): kernel_total, gain_total = lax.psum((kernel_term, gain_term), ('rep', 'dp'))  155 us
    psum x1, blocking collectives, body(): kernel_total, gain_total = lax.psum((kernel_term, gain_term), ('rep', 'dp'))  143 us
    all_to_all x1, waiting for transfers between devices, to_sources(): lax.all_to_all(outgoing, 'dp', split_axis=0, concat_axis=0, tiled=True)  19.9 us
  transfers between devices with their start and end apart: 5, of which 4 were waited for; matrix products, arithmetic and copies ran while one was open for 5% of the time, Pallas kernels for 0%

commit v1 on v0

--- a/solution.py
+++ b/solution.py
@@ -101,7 +101,9 @@
     updated = adam_step(master, moment, second, gradient)
     bucket = updated.astype(jnp.bfloat16)
     bucket_rows = bucket.shape[0]
-    gathered = lax.all_gather(bucket, "dp", axis=0, tiled=True)
+    gathered = jnp.concatenate(
+        lax.all_to_all(jnp.stack([bucket] * lax.axis_size("dp")), "dp", 0, 0), axis=0
+    )
     weight = jnp.take(gathered.reshape(owners, bucket_rows, columns), bucket_order, axis=0).reshape(
         owners * bucket_rows, columns
     )

time: 659 us -> 514 us (0.78)
  waiting for transfers between devices: 385 us -> 269 us
  blocking collectives: 143 us -> 109 us
    all_gather x1 -> x0, waiting for transfers between devices: 207 us -> none  [body(): gathered = lax.all_gather(bucket, 'dp', axis=0, tiled=True)]
    all_to_all x0 -> x1, waiting for transfers between devices: none -> 87.5 us  [body(): lax.all_to_all(jnp.stack([bucket] * lax.axis_size('dp')), 'dp', 0, 0)]
    psum x1, blocking collectives: 143 us -> 109 us  [body(): kernel_total, gain_total = lax.psum((kernel_term, gain_term), ('rep', 'dp'))]
    all_to_all x0 -> x1, starting transfers between devices: none -> 6.7 us  [body(): lax.all_to_all(jnp.stack([bucket] * lax.axis_size('dp')), 'dp', 0, 0)]
where the time goes in v1:
time: 514 us; the launch traced here: 513 us
  waiting for transfers between devices  269 us (52%)
  blocking collectives  109 us (21%)
  other arithmetic  39.4 us (8%)
  local copies, waits for them, and re-layouts  36.8 us (7%)
  starting transfers between devices  33.8 us (7%)
  between operations  15.4 us (3%)
  matrix products  9.28 us (2%)
    psum x1, waiting for transfers between devices, body(): kernel_total, gain_total = lax.psum((kernel_term, gain_term), ('rep', 'dp'))  153 us
    psum x1, blocking collectives, body(): kernel_total, gain_total = lax.psum((kernel_term, gain_term), ('rep', 'dp'))  109 us
    all_to_all x1, waiting for transfers between devices, body(): lax.all_to_all(jnp.stack([bucket] * lax.axis_size('dp')), 'dp', 0, 0)  87.5 us
    all_to_all x1, waiting for transfers between devices, to_sources(): lax.all_to_all(outgoing, 'dp', split_axis=0, concat_axis=0, tiled=True)  20.4 us
    all_to_all x1, starting transfers between devices, to_owners(): lax.all_to_all(has_block, 'dp', split_axis=0, concat_axis=0, tiled=True)  12.9 us
    unnamed x206, local copies, waits for them, and re-layouts  12.9 us
  transfers between devices with their start and end apart: 5, of which 4 were waited for; matrix products, arithmetic and copies ran while one was open for 5% of the time, Pallas kernels for 0%

profile of v1, /device:TPU:1, one launch (start us, length us, event | category | flops | bytes accessed | tf_op | source)
XLA Modules:
  0.0 513.3 jit_solution(4941417353320936954)
XLA Ops:
  8.6 12.9 %all-to-all-start = ((bf16[64,1,1]{2,1,0:T(2,128)(2,1)}), bf16[64,1,1]{2,1,0:T(2,128)(2,1)S(1)}, u32[]{:S(2)}, u32[]{:S(2)}) async-start(bf16[64,1,1]{2,1,0:T(2,128)(2,1)} %copy.26), calls=%async_computation | async-start | bytes 65536 | tf_op jit(solution)/shard_map/all_to_all | solution.py:57
  22.9 7.9 %all-to-all-done = bf16[64,1,1]{2,1,0:T(2,128)(2,1)S(1)} async-done(((bf16[64,1,1]{2,1,0:T(2,128)(2,1)}), bf16[64,1,1]{2,1,0:T(2,128)(2,1)S(1)}, u32[]{:S(2)}, u32[]{:S(2)}) %all-to-all-start) | async-done | bytes 160 | tf_op jit(solution)/shard_map/all_to_all | solution.py:57
  36.5 4.6 all-to-all-start.3
  42.0 20.4 %all-to-all-done.3 = bf16[64,2,3072]{2,1,0:T(2,128)(2,1)S(1)} async-done(((bf16[64,2,3072]{2,1,0:T(2,128)(2,1)}), bf16[64,2,3072]{2,1,0:T(2,128)(2,1)S(1)}, u32[]{:S(2)}, u32[]{:S(2)}) %all-to-all-start.3) | async-done | bytes 786464 | tf_op jit(solution)/shard_map/all_to_all | solution.py:79
  62.4 2.4 stack.2
  64.8 6.7 %all-to-all-start.1 = ((bf16[64,24,1536]{2,1,0:T(8,128)(2,1)}), bf16[64,24,1536]{2,1,0:T(8,128)(2,1)}, u32[]{:S(2)}, u32[]{:S(2)}) async-start(bf16[64,24,1536]{2,1,0:T(8,128)(2,1)} %stack.2), calls=%async_computation.1 | async-start | bytes 9437184 | tf_op jit(solution)/shard_map/all_to_all | solution.py:105
  75.3 3.9 fusion.26
  80.3 2.0 reshape.311
  82.3 2.1 convolution_convert_fusion.2
  84.8 87.5 %all-to-all-done.1 = bf16[64,24,1536]{2,1,0:T(8,128)(2,1)} async-done(((bf16[64,24,1536]{2,1,0:T(8,128)(2,1)}), bf16[64,24,1536]{2,1,0:T(8,128)(2,1)}, u32[]{:S(2)}, u32[]{:S(2)}) %all-to-all-start.1) | async-done | bytes 4718624 | tf_op jit(solution)/shard_map/all_to_all | solution.py:105
  172.3 5.4 %gather_fusion = bf16[64,24,1536]{2,1,0:T(8,128)(2,1)} fusion(bf16[64,24,1536]{2,1,0:T(8,128)(2,1)} %all-to-all-done.1, s32[1024]{0:T(1024)} %pad_clamp_fusion), kind=kCustom, calls=%fused_computation | custom fusion | bytes 9437440 | tf_op jit(solution)/shard_map/jit(_take)/gather | solution.py:107
  177.8 2.9 broadcast_select_fusion
  180.7 2.6 multiply_reduce_fusion
  184.2 3.6 multiply_reduce_fusion.15
  187.9 4.3 multiply_reduce_fusion.5
  192.3 4.6 multiply_multiply_fusion.13
  197.8 2.0 convolution_convert_fusion.5
  199.9 2.3 reshape.262
  211.0 3.2 reshape.308
  214.2 9.5 %all-to-all-start.2 = ((bf16[64,2,3072]{2,1,0:T(2,128)(2,1)}), bf16[64,2,3072]{2,1,0:T(2,128)(2,1)}, u32[]{:S(2)}, u32[]{:S(2)}) async-start(bf16[64,2,3072]{2,1,0:T(2,128)(2,1)} %reshape.308), calls=%async_computation.2 | async-start | bytes 1572864 | tf_op jit(solution)/shard_map/all_to_all | solution.py:56
  228.2 109.4 %psum.15 = f32[1536]{0:T(1024)S(1)} all-reduce(f32[1536]{0:T(1024)} %get-tuple-element.5), channel_id=1, replica_groups=mesh['rep'=8,'dp'=64] {'rep','dp'}, use_global_device_ids=true, to_apply=%region_26.27 | all-reduce | flops 1536 | bytes 12288 | tf_op jit(solution)/shard_map/psum | solution.py:137
  337.7 5.0 pad_add_fusion
  345.1 153.3 %all-reduce.34.cloned.1.call-done = f32[15,1536]{1,0:T(8,128)} async-done(((f32[15,1536]{1,0:T(8,128)}), f32[15,1536]{1,0:T(8,128)}) %all-reduce.34.cloned.1.call-update) | async-done | bytes 92176 | tf_op jit(solution)/shard_map/psum | solution.py:137
  499.9 4.9 reshape.309
  (262 shorter events, 34.3 us)
Async XLA Ops:
  8.6 22.2 %all-to-all-start = ((bf16[64,1,1]{2,1,0:T(2,128)(2,1)}), bf16[64,1,1]{2,1,0:T(2,128)(2,1)S(1)}, u32[]{:S(2)}, u32[]{:S(2)}) async-start(bf16[64,1,1]{2,1,0:T(2,128)(2,1)} %copy.26), calls=%async_computation | async-start | bytes 65536 | tf_op jit(solution)/shard_map/all_to_all | solution.py:57
  21.6 11.8 %copy-start.93 = (f32[32]{0:T(128)}, f32[32]{0:T(128)S(1)}, u32[]{:S(2)}) copy-start(f32[32]{0:T(128)S(1)} %iota_convert_fusion) | copy-start | bytes 388
  35.0 6.2 %copy-start.8 = (f32[24,1536]{1,0:T(8,128)S(1)}, f32[24,1536]{1,0:T(8,128)}, u32[]{:S(2)}) copy-start(f32[24,1536]{1,0:T(8,128)} %param.16) | copy-start | bytes 442372
  35.0 6.1 %copy-start.9 = (f32[24,1536]{1,0:T(8,128)S(1)}, f32[24,1536]{1,0:T(8,128)}, u32[]{:S(2)}) copy-start(f32[24,1536]{1,0:T(8,128)} %param.19) | copy-start | bytes 442372
  35.0 6.1 %copy-start.10 = (f32[24,1536]{1,0:T(8,128)S(1)}, f32[24,1536]{1,0:T(8,128)}, u32[]{:S(2)}) copy-start(f32[24,1536]{1,0:T(8,128)} %param.18) | copy-start | bytes 442372
  35.0 6.1 %copy-start.11 = (f32[24,1536]{1,0:T(8,128)S(1)}, f32[24,1536]{1,0:T(8,128)}, u32[]{:S(2)}) copy-start(f32[24,1536]{1,0:T(8,128)} %param.17) | copy-start | bytes 442372
  36.5 25.9 %all-to-all-start.3 = ((bf16[64,2,3072]{2,1,0:T(2,128)(2,1)}), bf16[64,2,3072]{2,1,0:T(2,128)(2,1)S(1)}, u32[]{:S(2)}, u32[]{:S(2)}) async-start(bf16[64,2,3072]{2,1,0:T(2,128)(2,1)} %reshape.310), calls=%async_computation.3 | async-start | bytes 1572864 | tf_op jit(solution)/shard_map/all_to_all | solution.py:79
  64.8 6.7 %copy-start.97 = (s32[1,8]{1,0:T(1,128)S(1)}, s32[1,8]{1,0:T(1,128)}, u32[]{:S(2)}) copy-start(s32[1,8]{1,0:T(1,128)} %param.12) | copy-start | bytes 100
  64.8 7.5 %copy-start.98 = (s32[64]{0:T(128)S(1)}, s32[64]{0:T(128)}, u32[]{:S(2)}) copy-start(s32[64]{0:T(128)} %param.20) | copy-start | bytes 772
  64.8 8.3 %copy-start.6 = (bf16[192,1536]{1,0:T(8,128)(2,1)S(1)}, bf16[192,1536]{1,0:T(8,128)(2,1)}, u32[]{:S(2)}) copy-start(bf16[192,1536]{1,0:T(8,128)(2,1)} %param.11) | copy-start | bytes 1769476
  64.8 107.5 %all-to-all-start.1 = ((bf16[64,24,1536]{2,1,0:T(8,128)(2,1)}), bf16[64,24,1536]{2,1,0:T(8,128)(2,1)}, u32[]{:S(2)}, u32[]{:S(2)}) async-start(bf16[64,24,1536]{2,1,0:T(8,128)(2,1)} %stack.2), calls=%async_computation.1 | async-start | bytes 9437184 | tf_op jit(solution)/shard_map/all_to_all | solution.py:105
  84.8 93.0 %copy-start.96 = (pred[64]{0:T(512)(128)(4,1)S(1)}, pred[64]{0:T(512)(128)(4,1)}, u32[]{:S(2)}) copy-start(pred[64]{0:T(512)(128)(4,1)} %copy-done.95) | copy-start | bytes 196
  187.9 9.0 %slice-start = ((s8[4718592]{0:T(1024)(128)(4,1)}), s8[4194304]{0:T(1024)(128)(4,1)S(1)}, s32[]{:S(2)}) async-start(s8[4718592]{0:T(1024)(128)(4,1)} %bitcast.24), calls=%async_computation.5 | async-start | bytes 8388608
  199.8 5.4 %copy-start.44 = (f32[1536]{0:T(1024)S(1)}, f32[1536]{0:T(1024)}, u32[]{:S(2)}) copy-start(f32[1536]{0:T(1024)} %get-tuple-element.12) | copy-start | bytes 18436
  199.9 6.0 %copy-start.43 = (f32[1536]{0:T(1024)S(1)}, f32[1536]{0:T(1024)}, u32[]{:S(2)}) copy-start(f32[1536]{0:T(1024)} %get-tuple-element.13) | copy-start | bytes 18436
  199.9 6.6 %copy-start.42 = (f32[1536]{0:T(1024)S(1)}, f32[1536]{0:T(1024)}, u32[]{:S(2)}) copy-start(f32[1536]{0:T(1024)} %get-tuple-element.14) | copy-start | bytes 18436
  199.9 7.2 %copy-start.41 = (f32[1536]{0:T(1024)S(1)}, f32[1536]{0:T(1024)}, u32[]{:S(2)}) copy-start(f32[1536]{0:T(1024)} %get-tuple-element.15) | copy-start | bytes 18436
  199.9 7.8 %copy-start.92 = (s32[1,48]{1,0:T(1,128)S(1)}, s32[1,48]{1,0:T(1,128)}, u32[]{:S(2)}) copy-start(s32[1,48]{1,0:T(1,128)} %param.13) | copy-start | bytes 580
  214.2 12.3 %copy-start.40 = (f32[1536]{0:T(1024)S(1)}, f32[1536]{0:T(1024)}, u32[]{:S(2)}) copy-start(f32[1536]{0:T(1024)} %get-tuple-element.20) | copy-start | bytes 18436
  214.2 12.3 %copy-start.39 = (f32[1536]{0:T(1024)S(1)}, f32[1536]{0:T(1024)}, u32[]{:S(2)}) copy-start(f32[1536]{0:T(1024)} %get-tuple-element.22) | copy-start | bytes 18436
  214.2 123.4 %copy-start = (f32[192,1536]{1,0:T(8,128)S(1)}, f32[192,1536]{1,0:T(8,128)}, u32[]{:S(2)}) copy-start(f32[192,1536]{1,0:T(8,128)} %get-tuple-element.50) | copy-start | bytes 3538948
  214.2 285.7 %all-to-all-start.2 = ((bf16[64,2,3072]{2,1,0:T(2,128)(2,1)}), bf16[64,2,3072]{2,1,0:T(2,128)(2,1)}, u32[]{:S(2)}, u32[]{:S(2)}) async-start(bf16[64,2,3072]{2,1,0:T(2,128)(2,1)} %reshape.308), calls=%async_computation.2 | async-start | bytes 1572864 | tf_op jit(solution)/shard_map/all_to_all | solution.py:56
  223.7 274.7 %all-reduce.34.cloned.1.call-start = ((), (), s32[]{:S(2)}) async-start(), calls=%async_computation.4 | async-start | bytes 196608 | tf_op jit(solution)/shard_map/psum | solution.py:137
  337.7 5.1 copy-start.5
  (82 other events, 297.4 us)
Sparse Core Ops, SparseCore 0:
  230.1 268.2 all-reduce.33
